TPU v7x, 32 devices: a whole 2x2x4 slice. The times are simulated.
32 devices in a mesh: ra: 4 (over x, core), rb: 8 (over z, y).
Axes of the slice: x: 2, y: 2, z: 4, core: 2. Of those that a mesh axis runs over, the one named last changes fastest.
Arguments:
- amplitude: bfloat16 [2, 512, 512, 256], P(None, 'ra', 'rb'), may hold values from -6 to 6
- coupling: bfloat16 [6, 256, 256], replicated, may hold values from -0.5 to 0.5
- pattern: int32 [6, 4, 4], replicated, may hold values 0 or 1
- radial: float32 [6, 512, 512], P(None, 'ra', 'rb'), may hold values from -2.4 to 2.4
- first_prop: bfloat16 [2, 512, 512], replicated, may hold values from -0.1875 to 0.1875
- second_prop: bfloat16 [2, 512, 512], replicated, may hold values from -0.1875 to 0.1875
Outputs:
- evolved: bfloat16 [2, 512, 512, 256], P(None, 'ra', 'rb')
All inputs are finite; a program needn't handle non-finite values.
Results may differ from a plain program's by a relative error of at most 0.0095.
Values may be sent and summed in bfloat16 or wider, within the bound.
A program may use at most 128 MiB of HBM per device.

v0:
```python
import jax
import jax.numpy as jnp
from jax import lax
from jax.sharding import PartitionSpec as P

KTERMS = 6
STEPS = 2


def complex_rows(matrix, piece):
    form = "ac,cqw->aqw"
    real_part = jnp.einsum(
        form, matrix[0], piece[0], preferred_element_type=jnp.float32
    ) - jnp.einsum(form, matrix[1], piece[1], preferred_element_type=jnp.float32)
    imag_part = jnp.einsum(
        form, matrix[0], piece[1], preferred_element_type=jnp.float32
    ) + jnp.einsum(form, matrix[1], piece[0], preferred_element_type=jnp.float32)
    return jnp.stack([real_part, imag_part]).astype(jnp.bfloat16)


def on_device(amplitude, coupling, pattern, radial, first_prop, second_prop):
    first_rows, second_rows, channels = (amplitude.shape[1], amplitude.shape[2], amplitude.shape[3])
    cells = first_rows * second_rows
    count = pattern.shape[1]
    block_size = channels // count
    groups_a = lax.axis_size("ra")
    groups_b = lax.axis_size("rb")
    width_a = channels // groups_a
    width_b = channels // groups_b
    spread = jnp.broadcast_to(
        pattern[:, :, None, :, None], (KTERMS, count, block_size, count, block_size)
    )
    block_mask = spread.reshape(KTERMS, channels, channels).astype(jnp.bfloat16)
    weights = coupling * block_mask
    radial_cells = radial.reshape(KTERMS, cells).T
    for sweep in range(STEPS):
        flat = amplitude.reshape(2 * cells, channels)
        applied = jnp.einsum("mj,kij->mki", flat, weights, preferred_element_type=jnp.float32)
        applied = applied.reshape(2, cells, KTERMS, channels)
        coupled = jnp.sum(applied * radial_cells[None, :, :, None], axis=2)
        wide = amplitude.reshape(2, cells, channels).astype(jnp.float32)
        kicked = jnp.stack([wide[0] + coupled[1], wide[1] - coupled[0]]).astype(jnp.bfloat16)
        grouped = kicked.reshape(2, first_rows, second_rows, groups_a, width_a)
        grouped = grouped.transpose(0, 1, 3, 2, 4).reshape(
            2, first_rows, groups_a, second_rows * width_a
        )
        half = complex_rows(
            first_prop, lax.all_to_all(grouped, "ra", split_axis=2, concat_axis=1, tiled=True)
        )
        restored = lax.all_to_all(half, "ra", split_axis=1, concat_axis=2, tiled=True)
        restored = restored.reshape(2, first_rows, groups_a, second_rows, width_a)
        restored = restored.transpose(0, 1, 3, 2, 4).reshape(
            2, first_rows, second_rows, groups_b, width_b
        )
        regrouped = restored.transpose(0, 2, 3, 1, 4).reshape(
            2, second_rows, groups_b, first_rows * width_b
        )
        moved = complex_rows(
            second_prop, lax.all_to_all(regrouped, "rb", split_axis=2, concat_axis=1, tiled=True)
        )
        settled = lax.all_to_all(moved, "rb", split_axis=1, concat_axis=2, tiled=True)
        settled = settled.reshape(2, second_rows, groups_b, first_rows, width_b)
        amplitude = settled.transpose(0, 3, 1, 2, 4).reshape(2, first_rows, second_rows, channels)
    return amplitude


def solution(mesh):
    return jax.shard_map(
        on_device,
        mesh=mesh,
        in_specs=(P(None, "ra", "rb", None), P(), P(), P(None, "ra", "rb"), P(), P()),
        out_specs=P(None, "ra", "rb", None),
        check_vma=False,
    )
```

profile of v0, /device:TPU:0, one launch (start us, length us, event | category | flops | bytes accessed | tf_op | source)
XLA Modules:
  0.0 1957.4 jit_solution(6471844927591130573)
XLA Ops:
  34.3 23.9 %fusion = f32[16384,256]{0,1:T(8,128)} fusion(f32[16384,6]{0,1:T(8,128)S(1)} %bitcast.242, bf16[16384,256,1]{1,0,2:T(8,128)(2,1)} %bitcast.213, bf16[6,256,256]{2,1,0:T(8,128)(2,1)S(1)} %copy-done.8, bf16[6,256,256]{2,1,0:T(8,128)(2,1)S(1)} %convert_element_type.56), kind=kOutput, calls=%fused_computation.1 | convolution fusion | flops 12931432448 | bytes 27131904 | tf_op jit(solution)/shard_map/mj,kij->mki/dot_general | solution.py:38
  58.2 15.1 fusion.6
  98.4 14.7 maximum_bitcast_fusion
  113.1 18.7 copy.168
  131.8 101.7 %all_to_all.120 = bf16[2,128,4,4096]{1,3,0,2:T(8,128)(2,1)} all-to-all(bf16[2,128,4,4096]{1,3,0,2:T(8,128)(2,1)} %bitcast.206), channel_id=1, replica_groups=mesh['ra'=4,'rb'=8] {'ra'}, dimensions={2} | all-to-all | bytes 16777216 | tf_op jit(solution)/shard_map/all_to_all | solution.py:48
  271.1 21.5 %copy.137 = bf16[2,512,1,4096]{3,0,2,1:T(2,128)(2,1)} copy(bf16[2,512,1,4096]{1,3,2,0:T(8,128)(2,1)} %pad_maximum_fusion) | data formatting | bytes 16777216 | tf_op jit(solution)/shard_map/stack | solution.py:18
  292.6 100.7 %all_to_all.121 = bf16[2,512,1,4096]{3,0,2,1:T(2,128)(2,1)} all-to-all(bf16[2,512,1,4096]{3,0,2,1:T(2,128)(2,1)} %copy.137), channel_id=1, replica_groups=mesh['ra'=4,'rb'=8] {'ra'}, dimensions={1} | all-to-all | bytes 16777216 | tf_op jit(solution)/shard_map/all_to_all | solution.py:50
  393.3 12.8 copy.138
  427.8 29.1 %copy.141 = bf16[2,64,8,128,32]{1,4,3,2,0:T(8,128)(2,1)} copy(bf16[2,64,8,128,32]{3,4,2,1,0:T(8,128)(2,1)} %bitcast.207) | data formatting | bytes 16777216 | tf_op jit(solution)/shard_map/transpose | solution.py:55
  457.0 15.8 copy.142
  472.8 190.0 %all_to_all.122 = bf16[2,64,8,4096]{3,1,0,2:T(8,128)(2,1)} all-to-all(bf16[2,64,8,4096]{3,1,0,2:T(8,128)(2,1)} %copy.142), channel_id=1, replica_groups=mesh['ra'=4,'rb'=8] {'rb'}, dimensions={2} | all-to-all | bytes 16777216 | tf_op jit(solution)/shard_map/all_to_all | solution.py:59
  696.3 21.5 %copy.144 = bf16[2,512,1,4096]{3,0,2,1:T(2,128)(2,1)} copy(bf16[2,512,1,4096]{1,3,2,0:T(8,128)(2,1)} %pad_maximum_fusion.1) | data formatting | bytes 16777216 | tf_op jit(solution)/shard_map/stack | solution.py:18
  723.3 182.0 %all-to-all-done.3 = bf16[2,512,1,4096]{3,0,2,1:T(2,128)(2,1)} async-done(((bf16[2,512,1,4096]{3,0,2,1:T(2,128)(2,1)}), bf16[2,512,1,4096]{3,0,2,1:T(2,128)(2,1)}, u32[]{:S(2)}, u32[]{:S(2)}) %all-to-all-start.3) | async-done | bytes 8388640 | tf_op jit(solution)/shard_map/all_to_all | solution.py:61
  905.3 12.8 copy.145
  918.1 15.5 copy.146
  933.7 17.5 copy.147
  951.2 22.5 %reshape_reshape.4 = bf16[2,8192,256]{1,2,0:T(8,128)(2,1)} reshape(bf16[2,128,64,8,32]{2,1,4,3,0:T(8,128)(2,1)} %copy.147) | data formatting | bytes 16777216 | tf_op jit(solution)/shard_map/reshape;reshape | solution.py:41
  985.7 33.8 %multiply_reduce_fusion = f32[2,8192,256]{2,1,0:T(8,128)} fusion(f32[8192,6]{0,1:T(8,128)S(1)} %bitcast.241, bf16[2,8192,256]{1,2,0:T(8,128)(2,1)} %reshape_reshape.4, bf16[6,256,256,1]{2,1,0,3:T(8,128)(2,1)S(1)} %fusion.84), kind=kOutput, calls=%fused_computation.2 | convolution fusion | flops 12931039232 | bytes 26148864 | tf_op jit(solution)/shard_map/mj,kij->mki/dot_general | solution.py:38
  1029.9 15.3 fusion.2
  1083.1 14.7 maximum_bitcast_fusion.1
  1097.8 18.7 copy.171
  1116.5 100.8 %all_to_all.123 = bf16[2,128,4,4096]{1,3,0,2:T(8,128)(2,1)} all-to-all(bf16[2,128,4,4096]{1,3,0,2:T(8,128)(2,1)} %bitcast.209), channel_id=1, replica_groups=mesh['ra'=4,'rb'=8] {'ra'}, dimensions={2} | all-to-all | bytes 16777216 | tf_op jit(solution)/shard_map/all_to_all | solution.py:48
  1254.8 21.5 %copy.155 = bf16[2,512,1,4096]{3,0,2,1:T(2,128)(2,1)} copy(bf16[2,512,1,4096]{1,3,2,0:T(8,128)(2,1)} %pad_maximum_fusion.2) | data formatting | bytes 16777216 | tf_op jit(solution)/shard_map/stack | solution.py:18
  1276.3 100.9 %all_to_all.124 = bf16[2,512,1,4096]{3,0,2,1:T(2,128)(2,1)} all-to-all(bf16[2,512,1,4096]{3,0,2,1:T(2,128)(2,1)} %copy.155), channel_id=1, replica_groups=mesh['ra'=4,'rb'=8] {'ra'}, dimensions={1} | all-to-all | bytes 16777216 | tf_op jit(solution)/shard_map/all_to_all | solution.py:50
  1377.3 12.8 copy.156
  1411.8 29.1 %copy.159 = bf16[2,64,8,128,32]{1,4,3,2,0:T(8,128)(2,1)} copy(bf16[2,64,8,128,32]{3,4,2,1,0:T(8,128)(2,1)} %bitcast.210) | data formatting | bytes 16777216 | tf_op jit(solution)/shard_map/transpose | solution.py:55
  1440.9 15.8 copy.160
  1456.7 188.9 %all_to_all.125 = bf16[2,64,8,4096]{3,1,0,2:T(8,128)(2,1)} all-to-all(bf16[2,64,8,4096]{3,1,0,2:T(8,128)(2,1)} %copy.160), channel_id=1, replica_groups=mesh['ra'=4,'rb'=8] {'rb'}, dimensions={2} | all-to-all | bytes 16777216 | tf_op jit(solution)/shard_map/all_to_all | solution.py:59
  1679.0 21.5 %copy.162 = bf16[2,512,1,4096]{3,0,2,1:T(2,128)(2,1)} copy(bf16[2,512,1,4096]{1,3,2,0:T(8,128)(2,1)} %pad_maximum_fusion.3) | data formatting | bytes 16777216 | tf_op jit(solution)/shard_map/stack | solution.py:18
  1700.6 188.5 %all_to_all.126 = bf16[2,512,1,4096]{3,0,2,1:T(2,128)(2,1)} all-to-all(bf16[2,512,1,4096]{3,0,2,1:T(2,128)(2,1)} %copy.162), channel_id=1, replica_groups=mesh['ra'=4,'rb'=8] {'rb'}, dimensions={1} | all-to-all | bytes 16777216 | tf_op jit(solution)/shard_map/all_to_all | solution.py:61
  1901.9 15.5 copy.164
  1917.4 27.6 %copy.165 = bf16[2,128,64,8,32]{1,4,3,2,0:T(8,128)(2,1)} copy(bf16[2,128,64,8,32]{2,4,1,3,0:T(8,128)(2,1)} %bitcast.204) | data formatting | bytes 16777216 | tf_op jit(solution)/shard_map/transpose | solution.py:63
  (75 shorter events, 335.3 us)
Async XLA Ops:
  2.1 0.7 copy-start.6
  4.5 29.8 %copy-start.4 = (bf16[6,256,256]{2,1,0:T(8,128)(2,1)}, bf16[6,256,256]{2,1,0:T(8,128)(2,1)S(1)}, u32[]{:S(2)}) copy-start(bf16[6,256,256]{2,1,0:T(8,128)(2,1)S(1)} %convert_element_type.56) | copy-start | bytes 2359300
  25.3 9.0 copy-start.8
  245.5 3.9 copy-start
  670.7 3.9 copy-start.2
  717.7 5.5 copy-start.5
  717.7 5.5 copy-start.9
  717.7 187.6 %all-to-all-start.3 = ((bf16[2,512,1,4096]{3,0,2,1:T(2,128)(2,1)}), bf16[2,512,1,4096]{3,0,2,1:T(2,128)(2,1)}, u32[]{:S(2)}, u32[]{:S(2)}) async-start(bf16[2,512,1,4096]{3,0,2,1:T(2,128)(2,1)} %copy.144), calls=%async_computation.3 | async-start | bytes 16777216 | tf_op jit(solution)/shard_map/all_to_all | solution.py:61
  973.7 12.0 copy-start.7
  1229.2 3.9 copy-start.1
  1653.5 3.9 copy-start.3
where the time goes:
time: 1980 us; the launch traced here: 1960 us
  blocking collectives  972 us (49%)
  local copies, waits for them, and re-layouts  583 us (29%)
  waiting for transfers between devices  182 us (9%)
  matrix products  114 us (6%)
  other arithmetic  102 us (5%)
    all_to_all x2, blocking collectives, on_device(): lax.all_to_all(regrouped, 'rb', split_axis=2, concat_axis=1, tiled=True)  379 us
    all_to_all x2, blocking collectives, on_device(): lax.all_to_all(grouped, 'ra', split_axis=2, concat_axis=1, tiled=True)  203 us
    all_to_all x2, blocking collectives, on_device(): lax.all_to_all(half, 'ra', split_axis=1, concat_axis=2, tiled=True)  202 us
    all_to_all x1, blocking collectives, on_device(): lax.all_to_all(moved, 'rb', split_axis=1, concat_axis=2, tiled=True)  189 us
    all_to_all x1, waiting for transfers between devices, on_device(): lax.all_to_all(moved, 'rb', split_axis=1, concat_axis=2, tiled=True)  182 us
    another operation x4, local copies, waits for them, and re-layouts, complex_rows(): return jnp.stack([real_part, imag_part]).astype(jnp.bfloat16)  86 us
    transpose x2, local copies, waits for them, and re-layouts, on_device(): restored.transpose(0, 2, 3, 1, 4)  58.3 us
    dot_general x2, matrix products, on_device(): jnp.einsum('mj,kij->mki', flat, weights, preferred_element_type=jnp.float32)  57.7 us
  transfers between devices with their start and end apart: 1, of which 1 were waited for; matrix products, arithmetic and copies ran while one was open for 0% of the time, Pallas kernels for 0%

commit v1 on v0

--- a/solution.py
+++ b/solution.py
@@ -47,7 +47,10 @@
         half = complex_rows(
             first_prop, lax.all_to_all(grouped, "ra", split_axis=2, concat_axis=1, tiled=True)
         )
-        restored = lax.all_to_all(half, "ra", split_axis=1, concat_axis=2, tiled=True)
+        restored = jnp.concatenate(
+            lax.all_to_all(jnp.stack(jnp.split(half, lax.axis_size("ra"), axis=1)), "ra", 0, 0),
+            axis=2,
+        )
         restored = restored.reshape(2, first_rows, groups_a, second_rows, width_a)
         restored = restored.transpose(0, 1, 3, 2, 4).reshape(
             2, first_rows, second_rows, groups_b, width_b

time: 1980 us -> 1900 us (0.960)
  local copies, waits for them, and re-layouts: 583 us -> 501 us
    all_to_all x4 -> x0, local copies, waits for them, and re-layouts: 49.5 us -> none  [on_device(): lax.all_to_all(half, 'ra', split_axis=1, concat_axis=2, tiled=True)]
    another operation x4 -> x2, local copies, waits for them, and re-layouts: 86 us -> 43 us  [complex_rows(): return jnp.stack([real_part, imag_part]).astype(jnp.bfloat16)]
    another operation x2 -> x6, local copies, waits for them, and re-layouts: 12.6 us -> 38.9 us  [the longest x2 19.6 us: on_device(): restored = restored.reshape(2, first_rows, groups_a, second_rows, width_a)]
    another operation x2 -> x6, other arithmetic: 30.4 us -> 44.9 us
where the time goes in v1:
time: 1900 us; the launch traced here: 1890 us
  blocking collectives  963 us (51%)
  local copies, waits for them, and re-layouts  501 us (26%)
  waiting for transfers between devices  182 us (10%)
  matrix products  120 us (6%)
  other arithmetic  114 us (6%)
    all_to_all x2, blocking collectives, on_device(): lax.all_to_all(regrouped, 'rb', split_axis=2, concat_axis=1, tiled=True)  379 us
    all_to_all x2, blocking collectives, on_device(): lax.all_to_all(grouped, 'ra', split_axis=2, concat_axis=1, tiled=True)  202 us
    all_to_all x2, blocking collectives, on_device(): lax.all_to_all(jnp.stack(jnp.split(half, lax.axis_size('ra'), axis=1)), '...  194 us
    all_to_all x1, blocking collectives, on_device(): lax.all_to_all(moved, 'rb', split_axis=1, concat_axis=2, tiled=True)  189 us
    all_to_all x1, waiting for transfers between devices, on_device(): lax.all_to_all(moved, 'rb', split_axis=1, concat_axis=2, tiled=True)  182 us
    transpose x2, local copies, waits for them, and re-layouts, on_device(): restored.transpose(0, 2, 3, 1, 4)  58.3 us
    dot_general x2, matrix products, on_device(): jnp.einsum('mj,kij->mki', flat, weights, preferred_element_type=jnp.float32)  57.7 us
    all_to_all x4, local copies, waits for them, and re-layouts, on_device(): lax.all_to_all(moved, 'rb', split_axis=1, concat_axis=2, tiled=True)  56.8 us
  transfers between devices with their start and end apart: 1, of which 1 were waited for; matrix products, arithmetic and copies ran while one was open for 0% of the time, Pallas kernels for 0%

profile of v1, /device:TPU:0, one launch (start us, length us, event | category | flops | bytes accessed | tf_op | source)
XLA Modules:
  0.0 1885.4 jit_solution(17733266962812431367)
XLA Ops:
  34.3 23.9 %fusion = f32[16384,256]{0,1:T(8,128)} fusion(f32[16384,6]{0,1:T(8,128)S(1)} %bitcast.262, bf16[16384,256,1]{1,0,2:T(8,128)(2,1)} %bitcast.235, bf16[6,256,256]{2,1,0:T(8,128)(2,1)S(1)} %copy-done.10, bf16[6,256,256]{2,1,0:T(8,128)(2,1)S(1)} %convert_element_type.56), kind=kOutput, calls=%fused_computation.1 | convolution fusion | flops 12931432448 | bytes 27131904 | tf_op jit(solution)/shard_map/mj,kij->mki/dot_general | solution.py:38
  58.2 15.1 fusion.8
  73.3 12.6 stack.84
  98.4 14.7 maximum_bitcast_fusion
  113.1 18.7 copy.153
  131.9 101.5 %all_to_all.100 = bf16[2,128,4,4096]{1,3,0,2:T(8,128)(2,1)} all-to-all(bf16[2,128,4,4096]{1,3,0,2:T(8,128)(2,1)} %bitcast.228), channel_id=1, replica_groups=mesh['ra'=4,'rb'=8] {'ra'}, dimensions={2} | all-to-all | bytes 16777216 | tf_op jit(solution)/shard_map/all_to_all | solution.py:48
  278.1 12.7 pad_maximum_fusion.2
  290.7 96.9 %all_to_all.101 = bf16[4,2,128,1,4096]{2,4,1,3,0:T(8,128)(2,1)} all-to-all(bf16[4,2,128,1,4096]{2,4,1,3,0:T(8,128)(2,1)S(1)} %pad_maximum_fusion.2), channel_id=1, replica_groups=mesh['ra'=4,'rb'=8] {'ra'}, dimensions={0} | all-to-all | bytes 16777216 | tf_op jit(solution)/shard_map/all_to_all | solution.py:51
  397.4 29.2 %copy.126 = bf16[2,64,8,128,32]{1,4,3,2,0:T(8,128)(2,1)} copy(bf16[2,64,8,128,32]{3,4,2,1,0:T(8,128)(2,1)} %bitcast.229) | data formatting | bytes 16777216 | tf_op jit(solution)/shard_map/transpose | solution.py:58
  426.5 15.8 copy.127
  442.3 189.8 %all_to_all.102 = bf16[2,64,8,4096]{3,1,0,2:T(8,128)(2,1)} all-to-all(bf16[2,64,8,4096]{3,1,0,2:T(8,128)(2,1)} %copy.127), channel_id=1, replica_groups=mesh['ra'=4,'rb'=8] {'rb'}, dimensions={2} | all-to-all | bytes 16777216 | tf_op jit(solution)/shard_map/all_to_all | solution.py:62
  665.6 21.5 %copy.129 = bf16[2,512,1,4096]{3,0,2,1:T(2,128)(2,1)} copy(bf16[2,512,1,4096]{1,3,2,0:T(8,128)(2,1)} %pad_maximum_fusion.3) | data formatting | bytes 16777216 | tf_op jit(solution)/shard_map/stack | solution.py:18
  692.7 182.0 %all-to-all-done.3 = bf16[2,512,1,4096]{3,0,2,1:T(2,128)(2,1)} async-done(((bf16[2,512,1,4096]{3,0,2,1:T(2,128)(2,1)}), bf16[2,512,1,4096]{3,0,2,1:T(2,128)(2,1)}, u32[]{:S(2)}, u32[]{:S(2)}) %all-to-all-start.3) | async-done | bytes 8388640 | tf_op jit(solution)/shard_map/all_to_all | solution.py:64
  874.8 12.8 copy.130
  887.6 15.6 copy.131
  903.1 17.5 copy.132
  920.6 22.5 %reshape_reshape.11 = bf16[2,8192,256]{1,2,0:T(8,128)(2,1)} reshape(bf16[2,128,64,8,32]{2,1,4,3,0:T(8,128)(2,1)} %copy.132) | data formatting | bytes 16777216 | tf_op jit(solution)/shard_map/reshape;reshape | solution.py:41
  955.2 33.8 %multiply_reduce_fusion = f32[2,8192,256]{2,1,0:T(8,128)} fusion(f32[8192,6]{0,1:T(8,128)S(1)} %bitcast.261, bf16[2,8192,256]{1,2,0:T(8,128)(2,1)} %reshape_reshape.11, bf16[6,256,256,1]{2,1,0,3:T(8,128)(2,1)S(1)} %fusion.90), kind=kOutput, calls=%fused_computation.2 | convolution fusion | flops 12931039232 | bytes 26148864 | tf_op jit(solution)/shard_map/mj,kij->mki/dot_general | solution.py:38
  999.5 15.3 fusion.4
  1021.2 12.6 stack.98
  1052.7 14.7 maximum_bitcast_fusion.1
  1067.4 18.7 copy.156
  1086.2 101.0 %all_to_all.103 = bf16[2,128,4,4096]{1,3,0,2:T(8,128)(2,1)} all-to-all(bf16[2,128,4,4096]{1,3,0,2:T(8,128)(2,1)} %bitcast.231), channel_id=1, replica_groups=mesh['ra'=4,'rb'=8] {'ra'}, dimensions={2} | all-to-all | bytes 16777216 | tf_op jit(solution)/shard_map/all_to_all | solution.py:48
  1233.1 96.9 %all_to_all.104 = bf16[4,2,128,1,4096]{2,4,1,3,0:T(8,128)(2,1)} all-to-all(bf16[4,2,128,1,4096]{2,4,1,3,0:T(8,128)(2,1)S(1)} %pad_maximum_fusion.4), channel_id=1, replica_groups=mesh['ra'=4,'rb'=8] {'ra'}, dimensions={0} | all-to-all | bytes 16777216 | tf_op jit(solution)/shard_map/all_to_all | solution.py:51
  1339.8 29.2 %copy.144 = bf16[2,64,8,128,32]{1,4,3,2,0:T(8,128)(2,1)} copy(bf16[2,64,8,128,32]{3,4,2,1,0:T(8,128)(2,1)} %bitcast.232) | data formatting | bytes 16777216 | tf_op jit(solution)/shard_map/transpose | solution.py:58
  1368.9 15.8 copy.145
  1384.7 188.7 %all_to_all.105 = bf16[2,64,8,4096]{3,1,0,2:T(8,128)(2,1)} all-to-all(bf16[2,64,8,4096]{3,1,0,2:T(8,128)(2,1)} %copy.145), channel_id=1, replica_groups=mesh['ra'=4,'rb'=8] {'rb'}, dimensions={2} | all-to-all | bytes 16777216 | tf_op jit(solution)/shard_map/all_to_all | solution.py:62
  1606.9 21.5 %copy.147 = bf16[2,512,1,4096]{3,0,2,1:T(2,128)(2,1)} copy(bf16[2,512,1,4096]{1,3,2,0:T(8,128)(2,1)} %pad_maximum_fusion.5) | data formatting | bytes 16777216 | tf_op jit(solution)/shard_map/stack | solution.py:18
  1628.4 188.5 %all_to_all.106 = bf16[2,512,1,4096]{3,0,2,1:T(2,128)(2,1)} all-to-all(bf16[2,512,1,4096]{3,0,2,1:T(2,128)(2,1)} %copy.147), channel_id=1, replica_groups=mesh['ra'=4,'rb'=8] {'rb'}, dimensions={1} | all-to-all | bytes 16777216 | tf_op jit(solution)/shard_map/all_to_all | solution.py:64
  1817.0 12.8 copy.148
  1829.8 15.6 copy.149
  1845.3 27.6 %copy.150 = bf16[2,128,64,8,32]{1,4,3,2,0:T(8,128)(2,1)} copy(bf16[2,128,64,8,32]{2,4,1,3,0:T(8,128)(2,1)} %bitcast.226) | data formatting | bytes 16777216 | tf_op jit(solution)/shard_map/transpose | solution.py:66
  (79 shorter events, 289.2 us)
Async XLA Ops:
  2.1 0.7 copy-start.8
  4.5 29.8 %copy-start.6 = (bf16[6,256,256]{2,1,0:T(8,128)(2,1)}, bf16[6,256,256]{2,1,0:T(8,128)(2,1)S(1)}, u32[]{:S(2)}) copy-start(bf16[6,256,256]{2,1,0:T(8,128)(2,1)S(1)} %convert_element_type.56) | copy-start | bytes 2359300
  25.3 9.0 copy-start.10
  245.3 3.9 copy-start.2
  266.2 2.0 copy-start
  640.1 3.9 copy-start.4
  687.1 5.5 copy-start.7
  687.1 5.5 copy-start.11
  687.1 187.6 %all-to-all-start.3 = ((bf16[2,512,1,4096]{3,0,2,1:T(2,128)(2,1)}), bf16[2,512,1,4096]{3,0,2,1:T(2,128)(2,1)}, u32[]{:S(2)}, u32[]{:S(2)}) async-start(bf16[2,512,1,4096]{3,0,2,1:T(2,128)(2,1)} %copy.129), calls=%async_computation.3 | async-start | bytes 16777216 | tf_op jit(solution)/shard_map/all_to_all | solution.py:64
  943.2 12.0 copy-start.9
  1199.1 3.9 copy-start.3
  1219.9 2.0 copy-start.1
  1581.3 3.9 copy-start.5
